TPU v7x, 32 devices: a whole 2x2x4 slice. The times are simulated.
32 devices in a mesh: gx: 2 (over core), gy: 4 (over z), gz: 4 (over y, x).
Axes of the slice: x: 2, y: 2, z: 4, core: 2. Of those that a mesh axis runs over, the one named last changes fastest.
Arguments:
- density_volume: float32 [64, 512, 512], P('gz', 'gy', 'gx'), may hold values from -4 to 4
Outputs:
- colour: float32 [3, 512, 512], P(None, ('gy', 'gz'), 'gx')
- depth_map: float32 [512, 512], P(('gy', 'gz'), 'gx')
- transparency: float32 [512, 512], P(('gy', 'gz'), 'gx')
All inputs are finite; a program needn't handle non-finite values.
Results may differ from a plain program's by a relative error of at most 0.0003.
Values sent between devices are 32-bit elements; how exact they have to be, the bound alone decides.
No kernel may reach another device: no remote copies, remote signals or barrier semaphores. Data moves between devices by JAX's collectives and lax.ppermute only.
A program may use at most 128 MiB of HBM per device.

v0:
```python
import jax
import jax.numpy as jnp
from jax import lax
from jax.sharding import PartitionSpec as P


def with_halo(shard, sides, width):
    for axis, dim in sides:
        peers, length = (lax.axis_size(axis), shard.shape[dim])
        up = [(i, (i + 1) % peers) for i in range(peers - 1)]
        down = [(j, i) for i, j in up]
        last = lax.slice_in_dim(shard, length - width, length, axis=dim)
        initial = lax.slice_in_dim(shard, 0, width, axis=dim)
        before = lax.ppermute(last, axis, up)
        after = lax.ppermute(initial, axis, down)
        shard = jnp.concatenate([before, shard, after], axis=dim)
    return shard


def fourth(far_low, near_low, near_high, far_high):
    return (far_low - 8.0 * near_low + 8.0 * near_high - far_high) / 12.0


def shade(sample, grad_z, grad_y, grad_x):
    square = grad_z * grad_z + grad_y * grad_y + grad_x * grad_x
    facing = (0.64 * grad_z + 0.6 * grad_y + 0.48 * grad_x) * lax.rsqrt(square + 1.0)
    diffuse = 0.3 + 0.7 * jnp.maximum(facing, 0.0)
    edge_gain = 1.0 + square / (square + 1.0)
    density = jax.nn.softplus(sample) * edge_gain
    colour_red = jax.nn.sigmoid(2.0 * sample) * diffuse
    colour_green = jnp.exp(-0.5 * sample * sample) * diffuse
    colour_blue = jax.nn.sigmoid(-2.0 * sample) * diffuse
    return (density, colour_red, colour_green, colour_blue)


def blend_depth(received):
    through = received[4]
    running = jnp.cumprod(through, axis=0)
    front_pass = jnp.concatenate([jnp.ones_like(running[:1]), running[:-1]], axis=0)
    shaded = jnp.sum(front_pass[None] * received[:4], axis=1)
    return jnp.concatenate([shaded, running[-1:]], axis=0)


def on_device(density_volume):
    cells_z, cells_y, cells_x = density_volume.shape
    depth_count = lax.axis_size("gz")
    depth_index = lax.axis_index("gz")
    total_z = cells_z * depth_count
    depth_step = 2.0 / total_z
    padded = with_halo(density_volume, (("gx", 2), ("gy", 1), ("gz", 0)), 2)
    centre = padded[2:-2, 2:-2, 2:-2]
    grad_z = fourth(
        padded[0:-4, 2:-2, 2:-2],
        padded[1:-3, 2:-2, 2:-2],
        padded[3:-1, 2:-2, 2:-2],
        padded[4:, 2:-2, 2:-2],
    )
    grad_y = fourth(
        padded[2:-2, 0:-4, 2:-2],
        padded[2:-2, 1:-3, 2:-2],
        padded[2:-2, 3:-1, 2:-2],
        padded[2:-2, 4:, 2:-2],
    )
    grad_x = fourth(
        padded[2:-2, 2:-2, 0:-4],
        padded[2:-2, 2:-2, 1:-3],
        padded[2:-2, 2:-2, 3:-1],
        padded[2:-2, 2:-2, 4:],
    )
    density, colour_red, colour_green, colour_blue = shade(centre, grad_z, grad_y, grad_x)
    pixels = cells_y * cells_x
    optical = (density * depth_step).reshape(cells_z, pixels)
    row_iota = lax.broadcasted_iota(jnp.int32, (cells_z, cells_z), 0)
    col_iota = lax.broadcasted_iota(jnp.int32, (cells_z, cells_z), 1)
    lower_tri = (row_iota >= col_iota).astype(jnp.float32)
    inclusive = jnp.dot(
        lower_tri, optical, precision=lax.Precision.HIGHEST, preferred_element_type=jnp.float32
    )
    weight = jnp.exp(-(inclusive - optical)) * (1.0 - jnp.exp(-optical))
    depth_pos = (
        (depth_index * cells_z + jnp.arange(cells_z, dtype=jnp.int32)).astype(jnp.float32) + 0.5
    ) / total_z
    partial_value = jnp.stack(
        [
            jnp.sum(weight * colour_red.reshape(cells_z, pixels), axis=0),
            jnp.sum(weight * colour_green.reshape(cells_z, pixels), axis=0),
            jnp.sum(weight * colour_blue.reshape(cells_z, pixels), axis=0),
            jnp.sum(weight * depth_pos[:, None], axis=0),
            jnp.exp(-inclusive[-1]),
        ]
    ).reshape(5, cells_y, cells_x)
    piece_rows = cells_y // depth_count
    stacked = partial_value.reshape(5, depth_count, piece_rows, cells_x)
    final_image = blend_depth(
        lax.all_to_all(stacked, "gz", split_axis=1, concat_axis=1, tiled=True)
    )
    return (final_image[:3], final_image[3], final_image[4])


def solution(mesh):
    return jax.shard_map(
        on_device,
        mesh=mesh,
        in_specs=(P("gz", "gy", "gx"),),
        out_specs=(P(None, ("gy", "gz"), "gx"), P(("gy", "gz"), "gx"), P(("gy", "gz"), "gx")),
        check_vma=False,
    )
```

profile of v0, /device:TPU:0, one launch (start us, length us, event | category | flops | bytes accessed | tf_op | source)
XLA Modules:
  0.0 101.9 jit_solution(17254441752755021613)
XLA Ops:
  0.6 2.9 %fusion.27 = (f32[16,128,2]{2,1,0:T(8,128)}, f32[16,128,2]{2,1,0:T(8,128)S(1)}) fusion(f32[16,128,256]{2,1,0:T(8,128)} %param.1), kind=kLoop, calls=%fused_computation.73 | loop fusion | bytes 65536 | tf_op jit(solution)/shard_map/slice | solution.py:12
  3.5 1.7 %copy.11 = f32[16,128,2]{1,0,2:T(8,128)S(1)} copy(f32[16,128,2]{2,1,0:T(8,128)} %get-tuple-element.23) | data formatting | bytes 32768
  5.2 2.4 %collective-permute-start = (f32[16,128,2]{1,0,2:T(8,128)S(1)}, f32[16,128,2]{1,0,2:T(8,128)S(1)}, u32[]{:S(2)}, u32[]{:S(2)}) collective-permute-start(f32[16,128,2]{1,0,2:T(8,128)S(1)} %copy.11), channel_id=1, source_target_pairs={{0,16},{1,17},{2,18},{3,19},{4,20},{5,21},{6,22},{7,23},{8,24},{9,... | collective-permute-start | bytes 49160 | tf_op jit(solution)/shard_map/ppermute | solution.py:14
  7.9 1.3 %collective-permute-start.1 = (f32[16,128,2]{1,0,2:T(8,128)S(1)}, f32[16,128,2]{1,0,2:T(8,128)S(1)}, u32[]{:S(2)}, u32[]{:S(2)}) collective-permute-start(f32[16,128,2]{1,0,2:T(8,128)S(1)} %copy.12), channel_id=1, source_target_pairs={{16,0},{17,1},{18,2},{19,3},{20,4},{21,5},{22,6},{23,7},{24,8},{25... | collective-permute-start | bytes 49160 | tf_op jit(solution)/shard_map/ppermute | solution.py:15
  9.6 1.4 %collective-permute-done.1 = f32[16,128,2]{1,0,2:T(8,128)S(1)} collective-permute-done((f32[16,128,2]{1,0,2:T(8,128)S(1)}, f32[16,128,2]{1,0,2:T(8,128)S(1)}, u32[]{:S(2)}, u32[]{:S(2)}) %collective-permute-start.1) | collective-permute-done | bytes 16416 | tf_op jit(solution)/shard_map/ppermute | solution.py:15
  11.0 1.4 %copy.7 = f32[16,128,2]{2,1,0:T(8,128)} copy(f32[16,128,2]{1,0,2:T(8,128)S(1)} %collective-permute-done.1) | data formatting | bytes 32768 | tf_op jit(solution)/shard_map/ppermute | solution.py:15
  13.6 4.3 %collective-permute-start.2 = (f32[16,2,260]{2,1,0:T(2,128)S(1)}, f32[16,2,260]{2,1,0:T(2,128)S(1)}, u32[]{:S(2)}, u32[]{:S(2)}) collective-permute-start(f32[16,2,260]{2,1,0:T(2,128)S(1)} %get-tuple-element.20), channel_id=1, source_target_pairs={{0,4},{4,8},{8,12},{1,5},{5,9},{9,13},{2,6},{6,10},{10,14},{3,7},{... | collective-permute-start | bytes 99848 | tf_op jit(solution)/shard_map/ppermute | solution.py:14
  17.9 1.3 %collective-permute-start.3 = (f32[16,2,260]{2,1,0:T(2,128)S(1)}, f32[16,2,260]{2,1,0:T(2,128)S(1)}, u32[]{:S(2)}, u32[]{:S(2)}) collective-permute-start(f32[16,2,260]{2,1,0:T(2,128)S(1)} %get-tuple-element.21), channel_id=1, source_target_pairs={{4,0},{8,4},{12,8},{5,1},{9,5},{13,9},{6,2},{10,6},{14,10},{7,3},{... | collective-permute-start | bytes 99848 | tf_op jit(solution)/shard_map/ppermute | solution.py:15
  19.7 4.3 %collective-permute-done.3 = f32[16,2,260]{2,1,0:T(2,128)S(1)} collective-permute-done((f32[16,2,260]{2,1,0:T(2,128)S(1)}, f32[16,2,260]{2,1,0:T(2,128)S(1)}, u32[]{:S(2)}, u32[]{:S(2)}) %collective-permute-start.3) | collective-permute-done | bytes 33312 | tf_op jit(solution)/shard_map/ppermute | solution.py:15
  24.3 3.4 %collective-permute-start.4 = (f32[2,132,260]{2,1,0:T(8,128)S(1)}, f32[2,132,260]{2,1,0:T(8,128)S(1)}, u32[]{:S(2)}, u32[]{:S(2)}) collective-permute-start(f32[2,132,260]{2,1,0:T(8,128)S(1)} %get-tuple-element.14), channel_id=1, source_target_pairs={{0,1},{1,2},{2,3},{4,5},{5,6},{6,7},{8,9},{9,10},{10,11},{12,13},{... | collective-permute-start | bytes 823688 | tf_op jit(solution)/shard_map/ppermute | solution.py:14
  27.7 1.3 %collective-permute-start.5 = (f32[2,132,260]{2,1,0:T(8,128)S(1)}, f32[2,132,260]{2,1,0:T(8,128)S(1)}, u32[]{:S(2)}, u32[]{:S(2)}) collective-permute-start(f32[2,132,260]{2,1,0:T(8,128)S(1)} %get-tuple-element.15), channel_id=1, source_target_pairs={{1,0},{2,1},{3,2},{5,4},{6,5},{7,6},{9,8},{10,9},{11,10},{13,12},{... | collective-permute-start | bytes 823688 | tf_op jit(solution)/shard_map/ppermute | solution.py:15
  29.0 4.8 %maximum_maximum_fusion.1 = (f32[16,130,260]{2,1,0:T(8,128)}, f32[16,130,260]{2,1,0:T(8,128)}) fusion(f32[16,128,2]{2,1,0:T(8,128)S(1)} %copy-done.1, f32[16,128,256]{2,1,0:T(8,128)S(1)} %copy-done, f32[16,128,2]{2,1,0:T(8,128)S(1)} %copy.6, f32[16,2,260]{2,1,0:T(2,128)S(1)} %collective-permute-done.2, f32[16,2,260]{2,1,0:T(2,128)S(1)} %collective-permute-done.3), kind=kLoop, calls=%fused_computation.3 | loop fusion | flops 3244800 | bytes 6522880 | tf_op jit(solution)/shard_map/concatenate | solution.py:16
  33.8 1.7 %collective-permute-done.4 = f32[2,132,260]{2,1,0:T(8,128)S(1)} collective-permute-done((f32[2,132,260]{2,1,0:T(8,128)S(1)}, f32[2,132,260]{2,1,0:T(8,128)S(1)}, u32[]{:S(2)}, u32[]{:S(2)}) %collective-permute-start.4) | collective-permute-done | bytes 274592 | tf_op jit(solution)/shard_map/ppermute | solution.py:14
  35.5 10.9 %collective-permute-done.5 = f32[2,132,260]{2,1,0:T(8,128)S(1)} collective-permute-done((f32[2,132,260]{2,1,0:T(8,128)S(1)}, f32[2,132,260]{2,1,0:T(8,128)S(1)}, u32[]{:S(2)}, u32[]{:S(2)}) %collective-permute-start.5) | collective-permute-done | bytes 274592 | tf_op jit(solution)/shard_map/ppermute | solution.py:15
  46.4 6.6 %maximum_maximum_fusion = (f32[18,132,260]{2,1,0:T(8,128)}, f32[18,132,260]{2,1,0:T(8,128)}) fusion(f32[16,2,260]{2,1,0:T(2,128)S(1)} %collective-permute-done.3, f32[16,128,2]{2,1,0:T(8,128)S(1)} %copy-done.1, f32[16,128,256]{2,1,0:T(8,128)S(1)} %copy-done, f32[16,128,2]{2,1,0:T(8,128)S(1)} %copy.6, f32[16,2,260]{2,1,0:T(2,128)S(1)} %collective-permute-done.2, ...), kind=kLoop, calls=%fused_computation.1 | loop fusion | flops 6177600 | bytes 7687680 | tf_op jit(solution)/shard_map/concatenate | solution.py:16
  53.0 20.0 %divide_multiply_fusion.1 = (f32[16,128,256]{2,1,0:T(8,128)}, f32[16,128,256]{2,1,0:T(8,128)}, f32[16,128,256]{2,1,0:T(8,128)}, f32[16,128,256]{2,1,0:T(8,128)}, f32[16,128,256]{2,1,0:T(8,128)}) fusion(f32[16,128,256]{2,1,0:T(8,128)S(1)} %copy-done, f32[18,132,260]{2,1,0:T(8,128)} %get-tuple-element.13, f32[18,132,260]{2,1,0:T(8,128)} %get-tuple-element.12, ...), kind=kLoop, calls=%fused_computation.45 | loop fusion | flops 22020096 | bytes 29392896 | tf_op jit(solution)/shard_map/mul | solution.py:30
  73.0 5.2 %fusion.8 = (f32[16,128,256]{2,1,0:T(8,128)S(1)}, f32[16,128,256]{2,1,0:T(8,128)S(1)}, f32[16,128,256]{2,1,0:T(8,128)S(1)}) fusion(f32[16,128,256]{2,1,0:T(8,128)} %get-tuple-element.8, f32[16,128,256]{2,1,0:T(8,128)S(1)} %copy-done, f32[16,128,256]{2,1,0:T(8,128)} %get-tuple-element.11, f32[16,128,256]{2,1,0:T(8,128)} %get-tuple-element.10, ...), kind=kLoop, calls=%fused_computation.20 | loop fusion | flops 14155776 | bytes 16777216 | tf_op jit(solution)/shard_map/mul | solution.py:31
  78.2 1.2 %copy.16 = f32[2,8,128,256]{3,1,2,0:T(8,128)S(1)} copy(f32[2,8,128,256]{3,2,1,0:T(8,128)S(1)} %bitcast.24) | data formatting | bytes 4194304
  79.4 1.2 %copy.13 = f32[2,8,128,256]{3,1,2,0:T(8,128)S(1)} copy(f32[2,8,128,256]{3,2,1,0:T(8,128)S(1)} %bitcast.23) | data formatting | bytes 4194304
  80.6 1.2 %copy.15 = f32[2,8,128,256]{3,1,2,0:T(8,128)S(1)} copy(f32[2,8,128,256]{3,2,1,0:T(8,128)S(1)} %bitcast.22) | data formatting | bytes 4194304
  82.2 1.2 %copy.14 = f32[2,8,128,256]{3,1,2,0:T(8,128)S(1)} copy(f32[2,8,128,256]{3,2,1,0:T(8,128)S(1)} %bitcast.25) | data formatting | bytes 4194304
  83.4 4.5 %multiply_reduce_fusion = (f32[32768]{0:T(1024)S(1)}, f32[32768]{0:T(1024)S(1)}, f32[32768]{0:T(1024)S(1)}, f32[32768]{0:T(1024)S(1)}, f32[16,32768]{1,0:T(8,128)}) fusion(f32[16]{0:T(128)S(1)} %add_multiply_fusion, f32[16,32768]{1,0:T(8,128)S(1)} %bitcast.18, f32[16,32768]{1,0:T(8,128)S(1)} %bitcast.20, f32[16,32768]{1,0:T(8,128)S(1)} %bitcast.21, ...), kind=kOutput, calls=%fused_computation.40 | convolution fusion | flops 107348224 | bytes 11010112 | tf_op jit(solution)/shard_map/dot_general | solution.py:76
  88.1 1.7 %fusion.23 = f32[32768]{0:T(1024)S(1)} fusion(f32[16,32768]{1,0:T(8,128)} %get-tuple-element.27), kind=kLoop, calls=%fused_computation.59 | loop fusion | flops 32768 | bytes 262144 | tf_op jit(solution)/shard_map/exp | solution.py:89
  89.9 10.6 %all_to_all.5 = f32[5,4,32,256]{3,2,0,1:T(8,128)S(1)} all-to-all(f32[5,4,32,256]{3,2,0,1:T(8,128)S(1)} %bitcast_dynamic-update-slice_fusion), channel_id=1, replica_groups=mesh['gx'=2,'gy'=4,'gz'=4] {'gz'}, dimensions={1} | all-to-all | bytes 1310720 | tf_op jit(solution)/shard_map/all_to_all | solution.py:95
  (29 shorter events, 4.6 us)
Async XLA Ops:
  3.5 8.9 %copy-start = (f32[16,128,256]{2,1,0:T(8,128)S(1)}, f32[16,128,256]{2,1,0:T(8,128)}, u32[]{:S(2)}) copy-start(f32[16,128,256]{2,1,0:T(8,128)} %param.1) | copy-start | bytes 6291460
  5.2 4.0 %collective-permute-start = (f32[16,128,2]{1,0,2:T(8,128)S(1)}, f32[16,128,2]{1,0,2:T(8,128)S(1)}, u32[]{:S(2)}, u32[]{:S(2)}) collective-permute-start(f32[16,128,2]{1,0,2:T(8,128)S(1)} %copy.11), channel_id=1, source_target_pairs={{0,16},{1,17},{2,18},{3,19},{4,20},{5,21},{6,22},{7,23},{8,24},{9,... | collective-permute-start | bytes 49160 | tf_op jit(solution)/shard_map/ppermute | solution.py:14
  7.9 3.1 %collective-permute-start.1 = (f32[16,128,2]{1,0,2:T(8,128)S(1)}, f32[16,128,2]{1,0,2:T(8,128)S(1)}, u32[]{:S(2)}, u32[]{:S(2)}) collective-permute-start(f32[16,128,2]{1,0,2:T(8,128)S(1)} %copy.12), channel_id=1, source_target_pairs={{16,0},{17,1},{18,2},{19,3},{20,4},{21,5},{22,6},{23,7},{24,8},{25... | collective-permute-start | bytes 49160 | tf_op jit(solution)/shard_map/ppermute | solution.py:15
  12.5 11.5 %copy-start.1 = (f32[16,128,2]{2,1,0:T(8,128)S(1)}, f32[16,128,2]{2,1,0:T(8,128)}, u32[]{:S(2)}) copy-start(f32[16,128,2]{2,1,0:T(8,128)} %copy.7) | copy-start | bytes 49156
  13.6 6.1 %collective-permute-start.2 = (f32[16,2,260]{2,1,0:T(2,128)S(1)}, f32[16,2,260]{2,1,0:T(2,128)S(1)}, u32[]{:S(2)}, u32[]{:S(2)}) collective-permute-start(f32[16,2,260]{2,1,0:T(2,128)S(1)} %get-tuple-element.20), channel_id=1, source_target_pairs={{0,4},{4,8},{8,12},{1,5},{5,9},{9,13},{2,6},{6,10},{10,14},{3,7},{... | collective-permute-start | bytes 99848 | tf_op jit(solution)/shard_map/ppermute | solution.py:14
  17.9 6.0 %collective-permute-start.3 = (f32[16,2,260]{2,1,0:T(2,128)S(1)}, f32[16,2,260]{2,1,0:T(2,128)S(1)}, u32[]{:S(2)}, u32[]{:S(2)}) collective-permute-start(f32[16,2,260]{2,1,0:T(2,128)S(1)} %get-tuple-element.21), channel_id=1, source_target_pairs={{4,0},{8,4},{12,8},{5,1},{9,5},{13,9},{6,2},{10,6},{14,10},{7,3},{... | collective-permute-start | bytes 99848 | tf_op jit(solution)/shard_map/ppermute | solution.py:15
  24.3 11.2 %collective-permute-start.4 = (f32[2,132,260]{2,1,0:T(8,128)S(1)}, f32[2,132,260]{2,1,0:T(8,128)S(1)}, u32[]{:S(2)}, u32[]{:S(2)}) collective-permute-start(f32[2,132,260]{2,1,0:T(8,128)S(1)} %get-tuple-element.14), channel_id=1, source_target_pairs={{0,1},{1,2},{2,3},{4,5},{5,6},{6,7},{8,9},{9,10},{10,11},{12,13},{... | collective-permute-start | bytes 823688 | tf_op jit(solution)/shard_map/ppermute | solution.py:14
  27.7 18.7 %collective-permute-start.5 = (f32[2,132,260]{2,1,0:T(8,128)S(1)}, f32[2,132,260]{2,1,0:T(8,128)S(1)}, u32[]{:S(2)}, u32[]{:S(2)}) collective-permute-start(f32[2,132,260]{2,1,0:T(8,128)S(1)} %get-tuple-element.15), channel_id=1, source_target_pairs={{1,0},{2,1},{3,2},{5,4},{6,5},{7,6},{9,8},{10,9},{11,10},{13,12},{... | collective-permute-start | bytes 823688 | tf_op jit(solution)/shard_map/ppermute | solution.py:15
  80.6 1.6 %copy-start.2 = (f32[16,128,256]{2,1,0:T(8,128)S(1)}, f32[16,128,256]{2,1,0:T(8,128)}, u32[]{:S(2)}) copy-start(f32[16,128,256]{2,1,0:T(8,128)} %get-tuple-element.7) | copy-start | bytes 6291460
where the time goes:
time: 102 us
  other arithmetic  39.8 us (39%)
  waiting for transfers between devices  18.6 us (18%)
  starting transfers between devices  14 us (14%)
  local copies, waits for them, and re-layouts  13.5 us (13%)
  blocking collectives  10.6 us (10%)
  matrix products  4.45 us (4%)
    mul x1, other arithmetic, shade(): colour_red = jax.nn.sigmoid(2.0 * sample) * diffuse  20 us
    ppermute x3, waiting for transfers between devices, with_halo(): after = lax.ppermute(initial, axis, down)  16.5 us
    concatenate x2, other arithmetic, with_halo(): shard = jnp.concatenate([before, shard, after], axis=dim)  11.4 us
    all_to_all x1, blocking collectives, on_device(): lax.all_to_all(stacked, 'gz', split_axis=1, concat_axis=1, tiled=True)  10.6 us
    ppermute x3, starting transfers between devices, with_halo(): before = lax.ppermute(last, axis, up)  10.1 us
    unnamed x16, local copies, waits for them, and re-layouts  7.32 us
    mul x1, other arithmetic, shade(): colour_green = jnp.exp(-0.5 * sample * sample) * diffuse  5.18 us
    dot_general x1, matrix products, on_device(): jnp.dot(lower_tri, optical, precision=lax.Precision.HIGHEST, preferred_el...  4.45 us
  transfers between devices with their start and end apart: 6, of which 5 were waited for; matrix products, arithmetic and copies ran while one was open for 5% of the time, Pallas kernels for 0%

commit v1 on v0

--- a/solution.py
+++ b/solution.py
@@ -2,6 +2,13 @@
 import jax.numpy as jnp
 from jax import lax
 from jax.sharding import PartitionSpec as P
+
+
+def stacked_exchange(value, mesh_axis, split, join):
+    size = lax.axis_size(mesh_axis)
+    shards = jnp.stack(jnp.split(value, size, axis=split), axis=0)
+    shards = lax.all_to_all(shards, mesh_axis, split_axis=0, concat_axis=0)
+    return jnp.concatenate(shards, axis=join)
 
 
 def with_halo(shard, sides, width):
@@ -91,9 +98,7 @@
     ).reshape(5, cells_y, cells_x)
     piece_rows = cells_y // depth_count
     stacked = partial_value.reshape(5, depth_count, piece_rows, cells_x)
-    final_image = blend_depth(
-        lax.all_to_all(stacked, "gz", split_axis=1, concat_axis=1, tiled=True)
-    )
+    final_image = blend_depth(stacked_exchange(stacked, "gz", 1, 1))
     return (final_image[:3], final_image[3], final_image[4])
 
 

time: 102 us -> 99.7 us (0.977)
  matrix products: 4.45 us -> 3.07 us
  other arithmetic: 39.8 us -> 38.7 us
    dot_general x1, matrix products: 4.45 us -> 3.07 us  [on_device(): jnp.dot(lower_tri, optical, precision=lax.Precision.HIGHEST, preferred_el...]
    exp x1, other arithmetic: 1.65 us -> 0.42 us  [on_device(): jnp.exp(-inclusive[-1])]
  transfers between devices with their start and end apart: 6 -> 6, of which waited for: 5 -> 5; matrix products, arithmetic and copies ran while one was open for 5% -> 6% of each run, Pallas kernels for 0% -> 0%
where the time goes in v1:
time: 99.7 us; the launch traced here: 99.4 us
  other arithmetic  38.7 us (39%)
  waiting for transfers between devices  18.6 us (19%)
  starting transfers between devices  14 us (14%)
  local copies, waits for them, and re-layouts  13.6 us (14%)
  blocking collectives  10.6 us (11%)
  matrix products  3.07 us (3%)
    mul x1, other arithmetic, shade(): colour_red = jax.nn.sigmoid(2.0 * sample) * diffuse  20 us
    ppermute x3, waiting for transfers between devices, with_halo(): after = lax.ppermute(initial, axis, down)  16.5 us
    concatenate x2, other arithmetic, with_halo(): shard = jnp.concatenate([before, shard, after], axis=dim)  11.4 us
    all_to_all x1, blocking collectives, stacked_exchange(): shards = lax.all_to_all(shards, mesh_axis, split_axis=0, concat_axis=0)  10.6 us
    ppermute x3, starting transfers between devices, with_halo(): before = lax.ppermute(last, axis, up)  10.1 us
    unnamed x16, local copies, waits for them, and re-layouts  7.32 us
    mul x1, other arithmetic, shade(): colour_green = jnp.exp(-0.5 * sample * sample) * diffuse  5.18 us
    ppermute x3, starting transfers between devices, with_halo(): after = lax.ppermute(initial, axis, down)  3.88 us
  transfers between devices with their start and end apart: 6, of which 5 were waited for; matrix products, arithmetic and copies ran while one was open for 6% of the time, Pallas kernels for 0%

profile of v1, /device:TPU:0, one launch (start us, length us, event | category | flops | bytes accessed | tf_op | source)
XLA Modules:
  0.0 99.4 jit_solution(3125119165410540349)
XLA Ops:
  0.6 2.9 %fusion.28 = (f32[16,128,2]{2,1,0:T(8,128)}, f32[16,128,2]{2,1,0:T(8,128)S(1)}) fusion(f32[16,128,256]{2,1,0:T(8,128)} %param.1), kind=kLoop, calls=%fused_computation.79 | loop fusion | bytes 65536 | tf_op jit(solution)/shard_map/slice | solution.py:19
  3.5 1.7 %copy.18 = f32[16,128,2]{1,0,2:T(8,128)S(1)} copy(f32[16,128,2]{2,1,0:T(8,128)} %get-tuple-element.23) | data formatting | bytes 32768
  5.2 2.4 %collective-permute-start = (f32[16,128,2]{1,0,2:T(8,128)S(1)}, f32[16,128,2]{1,0,2:T(8,128)S(1)}, u32[]{:S(2)}, u32[]{:S(2)}) collective-permute-start(f32[16,128,2]{1,0,2:T(8,128)S(1)} %copy.18), channel_id=1, source_target_pairs={{0,16},{1,17},{2,18},{3,19},{4,20},{5,21},{6,22},{7,23},{8,24},{9,... | collective-permute-start | bytes 49160 | tf_op jit(solution)/shard_map/ppermute | solution.py:21
  7.9 1.3 %collective-permute-start.1 = (f32[16,128,2]{1,0,2:T(8,128)S(1)}, f32[16,128,2]{1,0,2:T(8,128)S(1)}, u32[]{:S(2)}, u32[]{:S(2)}) collective-permute-start(f32[16,128,2]{1,0,2:T(8,128)S(1)} %copy.19), channel_id=1, source_target_pairs={{16,0},{17,1},{18,2},{19,3},{20,4},{21,5},{22,6},{23,7},{24,8},{25... | collective-permute-start | bytes 49160 | tf_op jit(solution)/shard_map/ppermute | solution.py:22
  9.6 1.4 %collective-permute-done.1 = f32[16,128,2]{1,0,2:T(8,128)S(1)} collective-permute-done((f32[16,128,2]{1,0,2:T(8,128)S(1)}, f32[16,128,2]{1,0,2:T(8,128)S(1)}, u32[]{:S(2)}, u32[]{:S(2)}) %collective-permute-start.1) | collective-permute-done | bytes 16416 | tf_op jit(solution)/shard_map/ppermute | solution.py:22
  11.0 1.4 %copy.11 = f32[16,128,2]{2,1,0:T(8,128)} copy(f32[16,128,2]{1,0,2:T(8,128)S(1)} %collective-permute-done.1) | data formatting | bytes 32768 | tf_op jit(solution)/shard_map/ppermute | solution.py:22
  12.5 1.2 %pad_maximum_fusion.12 = (f32[16,2,260]{2,1,0:T(2,128)S(1)}, f32[16,2,260]{2,1,0:T(2,128)S(1)}) fusion(f32[16,128,2]{2,1,0:T(8,128)} %copy.11, f32[16,128,256]{2,1,0:T(8,128)S(1)} %copy-done, f32[16,128,2]{2,1,0:T(8,128)S(1)} %copy.10), kind=kLoop, calls=%fused_computation.69 | loop fusion | flops 33280 | bytes 2196480 | tf_op jit(solution)/shard_map/slice | solution.py:19
  13.6 4.3 %collective-permute-start.2 = (f32[16,2,260]{2,1,0:T(2,128)S(1)}, f32[16,2,260]{2,1,0:T(2,128)S(1)}, u32[]{:S(2)}, u32[]{:S(2)}) collective-permute-start(f32[16,2,260]{2,1,0:T(2,128)S(1)} %get-tuple-element.20), channel_id=1, source_target_pairs={{0,4},{4,8},{8,12},{1,5},{5,9},{9,13},{2,6},{6,10},{10,14},{3,7},{... | collective-permute-start | bytes 99848 | tf_op jit(solution)/shard_map/ppermute | solution.py:21
  17.9 1.3 %collective-permute-start.3 = (f32[16,2,260]{2,1,0:T(2,128)S(1)}, f32[16,2,260]{2,1,0:T(2,128)S(1)}, u32[]{:S(2)}, u32[]{:S(2)}) collective-permute-start(f32[16,2,260]{2,1,0:T(2,128)S(1)} %get-tuple-element.21), channel_id=1, source_target_pairs={{4,0},{8,4},{12,8},{5,1},{9,5},{13,9},{6,2},{10,6},{14,10},{7,3},{... | collective-permute-start | bytes 99848 | tf_op jit(solution)/shard_map/ppermute | solution.py:22
  19.7 4.3 %collective-permute-done.3 = f32[16,2,260]{2,1,0:T(2,128)S(1)} collective-permute-done((f32[16,2,260]{2,1,0:T(2,128)S(1)}, f32[16,2,260]{2,1,0:T(2,128)S(1)}, u32[]{:S(2)}, u32[]{:S(2)}) %collective-permute-start.3) | collective-permute-done | bytes 33312 | tf_op jit(solution)/shard_map/ppermute | solution.py:22
  24.3 3.4 %collective-permute-start.4 = (f32[2,132,260]{2,1,0:T(8,128)S(1)}, f32[2,132,260]{2,1,0:T(8,128)S(1)}, u32[]{:S(2)}, u32[]{:S(2)}) collective-permute-start(f32[2,132,260]{2,1,0:T(8,128)S(1)} %get-tuple-element.14), channel_id=1, source_target_pairs={{0,1},{1,2},{2,3},{4,5},{5,6},{6,7},{8,9},{9,10},{10,11},{12,13},{... | collective-permute-start | bytes 823688 | tf_op jit(solution)/shard_map/ppermute | solution.py:21
  27.7 1.3 %collective-permute-start.5 = (f32[2,132,260]{2,1,0:T(8,128)S(1)}, f32[2,132,260]{2,1,0:T(8,128)S(1)}, u32[]{:S(2)}, u32[]{:S(2)}) collective-permute-start(f32[2,132,260]{2,1,0:T(8,128)S(1)} %get-tuple-element.15), channel_id=1, source_target_pairs={{1,0},{2,1},{3,2},{5,4},{6,5},{7,6},{9,8},{10,9},{11,10},{13,12},{... | collective-permute-start | bytes 823688 | tf_op jit(solution)/shard_map/ppermute | solution.py:22
  29.0 4.8 %maximum_maximum_fusion.1 = (f32[16,130,260]{2,1,0:T(8,128)}, f32[16,130,260]{2,1,0:T(8,128)}) fusion(f32[16,128,2]{2,1,0:T(8,128)S(1)} %copy-done.1, f32[16,128,256]{2,1,0:T(8,128)S(1)} %copy-done, f32[16,128,2]{2,1,0:T(8,128)S(1)} %copy.10, f32[16,2,260]{2,1,0:T(2,128)S(1)} %collective-permute-done.2, f32[16,2,260]{2,1,0:T(2,128)S(1)} %collective-permute-done.3), kind=kLoop, calls=%fused_computation.3 | loop fusion | flops 3244800 | bytes 6522880 | tf_op jit(solution)/shard_map/concatenate | solution.py:23
  33.8 1.7 %collective-permute-done.4 = f32[2,132,260]{2,1,0:T(8,128)S(1)} collective-permute-done((f32[2,132,260]{2,1,0:T(8,128)S(1)}, f32[2,132,260]{2,1,0:T(8,128)S(1)}, u32[]{:S(2)}, u32[]{:S(2)}) %collective-permute-start.4) | collective-permute-done | bytes 274592 | tf_op jit(solution)/shard_map/ppermute | solution.py:21
  35.5 10.9 %collective-permute-done.5 = f32[2,132,260]{2,1,0:T(8,128)S(1)} collective-permute-done((f32[2,132,260]{2,1,0:T(8,128)S(1)}, f32[2,132,260]{2,1,0:T(8,128)S(1)}, u32[]{:S(2)}, u32[]{:S(2)}) %collective-permute-start.5) | collective-permute-done | bytes 274592 | tf_op jit(solution)/shard_map/ppermute | solution.py:22
  46.4 6.6 %maximum_maximum_fusion = (f32[18,132,260]{2,1,0:T(8,128)}, f32[18,132,260]{2,1,0:T(8,128)}) fusion(f32[16,2,260]{2,1,0:T(2,128)S(1)} %collective-permute-done.3, f32[16,128,2]{2,1,0:T(8,128)S(1)} %copy-done.1, f32[16,128,256]{2,1,0:T(8,128)S(1)} %copy-done, f32[16,128,2]{2,1,0:T(8,128)S(1)} %copy.10, f32[16,2,260]{2,1,0:T(2,128)S(1)} %collective-permute-done.2, ...), kind=kLoop, calls=%fused_computation.1 | loop fusion | flops 6177600 | bytes 7687680 | tf_op jit(solution)/shard_map/concatenate | solution.py:23
  53.0 20.0 %divide_multiply_fusion.1 = (f32[16,128,256]{2,1,0:T(8,128)}, f32[16,128,256]{2,1,0:T(8,128)}, f32[16,128,256]{2,1,0:T(8,128)}, f32[16,128,256]{2,1,0:T(8,128)}, f32[16,128,256]{2,1,0:T(8,128)}) fusion(f32[16,128,256]{2,1,0:T(8,128)S(1)} %copy-done, f32[18,132,260]{2,1,0:T(8,128)} %get-tuple-element.13, f32[18,132,260]{2,1,0:T(8,128)} %get-tuple-element.12, ...), kind=kLoop, calls=%fused_computation.45 | loop fusion | flops 22020096 | bytes 29392896 | tf_op jit(solution)/shard_map/mul | solution.py:37
  73.0 5.2 %fusion.8 = (f32[16,128,256]{2,1,0:T(8,128)S(1)}, f32[16,128,256]{2,1,0:T(8,128)S(1)}, f32[16,128,256]{2,1,0:T(8,128)S(1)}) fusion(f32[16,128,256]{2,1,0:T(8,128)} %get-tuple-element.8, f32[16,128,256]{2,1,0:T(8,128)S(1)} %copy-done, f32[16,128,256]{2,1,0:T(8,128)} %get-tuple-element.11, f32[16,128,256]{2,1,0:T(8,128)} %get-tuple-element.10, ...), kind=kLoop, calls=%fused_computation.20 | loop fusion | flops 14155776 | bytes 16777216 | tf_op jit(solution)/shard_map/mul | solution.py:38
  78.2 1.2 %copy.20 = f32[2,8,128,256]{3,1,2,0:T(8,128)S(1)} copy(f32[2,8,128,256]{3,2,1,0:T(8,128)S(1)} %bitcast.45) | data formatting | bytes 4194304
  79.4 1.2 %copy.22 = f32[2,8,128,256]{3,1,2,0:T(8,128)S(1)} copy(f32[2,8,128,256]{3,2,1,0:T(8,128)S(1)} %bitcast.44) | data formatting | bytes 4194304
  80.6 1.2 %copy.23 = f32[2,8,128,256]{3,1,2,0:T(8,128)S(1)} copy(f32[2,8,128,256]{3,2,1,0:T(8,128)S(1)} %bitcast.43) | data formatting | bytes 4194304
  82.2 1.2 %copy.21 = f32[2,8,128,256]{3,1,2,0:T(8,128)S(1)} copy(f32[2,8,128,256]{3,2,1,0:T(8,128)S(1)} %bitcast.46) | data formatting | bytes 4194304
  83.4 3.1 %multiply_reduce_fusion = (f32[32768]{0:T(1024)S(1)}, f32[32768]{0:T(1024)S(1)}, f32[32768]{0:T(1024)S(1)}, f32[32768]{0:T(1024)S(1)}, f32[16,32768]{1,0:T(8,128)S(1)}) fusion(f32[16]{0:T(128)S(1)} %add_multiply_fusion, f32[16,32768]{1,0:T(8,128)S(1)} %bitcast.41, f32[16,32768]{1,0:T(8,128)S(1)} %bitcast.40, f32[16,32768]{1,0:T(8,128)S(1)} %bitcast.42, ...), kind=kOutput, calls=%fused_computation.40 | convolution fusion | flops 107348224 | bytes 11010112 | tf_op jit(solution)/shard_map/dot_general | solution.py:83
  87.4 10.6 %all_to_all.5 = f32[4,5,1,32,256]{4,3,2,1,0:T(8,128)S(1)} all-to-all(f32[4,5,1,32,256]{4,3,2,1,0:T(8,128)S(1)} %pad_maximum_fusion.4), channel_id=1, replica_groups=mesh['gx'=2,'gy'=4,'gz'=4] {'gz'}, dimensions={0} | all-to-all | bytes 1310720 | tf_op jit(solution)/shard_map/all_to_all | solution.py:10
  (31 shorter events, 4.0 us)
Async XLA Ops:
  3.5 8.9 %copy-start = (f32[16,128,256]{2,1,0:T(8,128)S(1)}, f32[16,128,256]{2,1,0:T(8,128)}, u32[]{:S(2)}) copy-start(f32[16,128,256]{2,1,0:T(8,128)} %param.1) | copy-start | bytes 6291460
  5.2 4.0 %collective-permute-start = (f32[16,128,2]{1,0,2:T(8,128)S(1)}, f32[16,128,2]{1,0,2:T(8,128)S(1)}, u32[]{:S(2)}, u32[]{:S(2)}) collective-permute-start(f32[16,128,2]{1,0,2:T(8,128)S(1)} %copy.18), channel_id=1, source_target_pairs={{0,16},{1,17},{2,18},{3,19},{4,20},{5,21},{6,22},{7,23},{8,24},{9,... | collective-permute-start | bytes 49160 | tf_op jit(solution)/shard_map/ppermute | solution.py:21
  7.9 3.1 %collective-permute-start.1 = (f32[16,128,2]{1,0,2:T(8,128)S(1)}, f32[16,128,2]{1,0,2:T(8,128)S(1)}, u32[]{:S(2)}, u32[]{:S(2)}) collective-permute-start(f32[16,128,2]{1,0,2:T(8,128)S(1)} %copy.19), channel_id=1, source_target_pairs={{16,0},{17,1},{18,2},{19,3},{20,4},{21,5},{22,6},{23,7},{24,8},{25... | collective-permute-start | bytes 49160 | tf_op jit(solution)/shard_map/ppermute | solution.py:22
  12.5 11.5 %copy-start.1 = (f32[16,128,2]{2,1,0:T(8,128)S(1)}, f32[16,128,2]{2,1,0:T(8,128)}, u32[]{:S(2)}) copy-start(f32[16,128,2]{2,1,0:T(8,128)} %copy.11) | copy-start | bytes 49156
  13.6 6.1 %collective-permute-start.2 = (f32[16,2,260]{2,1,0:T(2,128)S(1)}, f32[16,2,260]{2,1,0:T(2,128)S(1)}, u32[]{:S(2)}, u32[]{:S(2)}) collective-permute-start(f32[16,2,260]{2,1,0:T(2,128)S(1)} %get-tuple-element.20), channel_id=1, source_target_pairs={{0,4},{4,8},{8,12},{1,5},{5,9},{9,13},{2,6},{6,10},{10,14},{3,7},{... | collective-permute-start | bytes 99848 | tf_op jit(solution)/shard_map/ppermute | solution.py:21
  17.9 6.0 %collective-permute-start.3 = (f32[16,2,260]{2,1,0:T(2,128)S(1)}, f32[16,2,260]{2,1,0:T(2,128)S(1)}, u32[]{:S(2)}, u32[]{:S(2)}) collective-permute-start(f32[16,2,260]{2,1,0:T(2,128)S(1)} %get-tuple-element.21), channel_id=1, source_target_pairs={{4,0},{8,4},{12,8},{5,1},{9,5},{13,9},{6,2},{10,6},{14,10},{7,3},{... | collective-permute-start | bytes 99848 | tf_op jit(solution)/shard_map/ppermute | solution.py:22
  24.3 11.2 %collective-permute-start.4 = (f32[2,132,260]{2,1,0:T(8,128)S(1)}, f32[2,132,260]{2,1,0:T(8,128)S(1)}, u32[]{:S(2)}, u32[]{:S(2)}) collective-permute-start(f32[2,132,260]{2,1,0:T(8,128)S(1)} %get-tuple-element.14), channel_id=1, source_target_pairs={{0,1},{1,2},{2,3},{4,5},{5,6},{6,7},{8,9},{9,10},{10,11},{12,13},{... | collective-permute-start | bytes 823688 | tf_op jit(solution)/shard_map/ppermute | solution.py:21
  27.7 18.7 %collective-permute-start.5 = (f32[2,132,260]{2,1,0:T(8,128)S(1)}, f32[2,132,260]{2,1,0:T(8,128)S(1)}, u32[]{:S(2)}, u32[]{:S(2)}) collective-permute-start(f32[2,132,260]{2,1,0:T(8,128)S(1)} %get-tuple-element.15), channel_id=1, source_target_pairs={{1,0},{2,1},{3,2},{5,4},{6,5},{7,6},{9,8},{10,9},{11,10},{13,12},{... | collective-permute-start | bytes 823688 | tf_op jit(solution)/shard_map/ppermute | solution.py:22
  80.6 1.6 %copy-start.2 = (f32[16,128,256]{2,1,0:T(8,128)S(1)}, f32[16,128,256]{2,1,0:T(8,128)}, u32[]{:S(2)}) copy-start(f32[16,128,256]{2,1,0:T(8,128)} %get-tuple-element.7) | copy-start | bytes 6291460
